TPU v7x, 256 devices: a whole 4x4x8 slice. The times are simulated.
256 devices in a mesh: dp: 16 (over y, z_hi), mp: 16 (over x, z_lo, core).
Axes of the slice: x: 4, y: 4, z: 8 (z_hi: 4, z_lo: 2; z = z_hi * 2 + z_lo), core: 2. Of those that a mesh axis runs over, the one named last changes fastest.
Arguments:
- tokens: bfloat16 [4096, 4096], P('dp', 'mp'), may hold values from -6 to 6
- norm_gain: float32 [4096], P('mp'), may hold values from 0.75 to 7.5
- w_gate: bfloat16 [4096, 6144], P('dp', 'mp'), may hold values from -0.09375 to 0.09375
- w_up: bfloat16 [4096, 6144], P('dp', 'mp'), may hold values from -0.09375 to 0.09375
- cotangent: bfloat16 [4096, 6144], P('dp', 'mp'), may hold values from -0.09375 to 0.09375
- decay_mask: int32 [2, 4096], replicated, may hold values 0 or 1
- radius: float32 [1], replicated, may hold values from 12.8 to 38.4
Outputs:
- grad_gain: float32 [4096], P('mp')
- grad_gate: float32 [4096, 6144], P('dp', 'mp')
- grad_up: float32 [4096, 6144], P('dp', 'mp')
Inputs may be any that keep to these rules, and one draw needn't show every extreme that they name: `decay_mask`: 1 marks a row that is perturbed.
All inputs are finite; a program needn't handle non-finite values.
Results may differ from a plain program's by a relative error of at most 0.024.
Values may be sent and summed in bfloat16 or wider, within the bound.
No kernel may reach another device: no remote copies, remote signals or barrier semaphores. Data moves between devices by JAX's collectives and lax.ppermute only.
A program may use at most 64 MiB of HBM per device.

v0:
```python
import jax
import jax.numpy as jnp
from jax import lax
from jax.sharding import PartitionSpec as P


def activation(value):
    return jax.nn.gelu(value, approximate=True)


def fetch_weights(part_gate, part_up):
    return (
        lax.all_gather(part_gate, "dp", axis=0, tiled=True),
        lax.all_gather(part_up, "dp", axis=0, tiled=True),
    )


def one_pass(scaled_rows, gain_part, full_gate, full_up, cotangent):
    hidden_width = full_gate.shape[1]
    normed_part = (scaled_rows * gain_part[None, :]).astype(jnp.bfloat16)
    normed = lax.all_gather(normed_part, "mp", axis=1, tiled=True)
    pre_gate = jnp.dot(normed, full_gate, preferred_element_type=jnp.float32)
    pre_up = jnp.dot(normed, full_up, preferred_element_type=jnp.float32)
    activated, back_fn = jax.vjp(activation, pre_gate)
    upstream = cotangent.astype(jnp.float32)
    d_up = (upstream * activated).astype(jnp.bfloat16)
    d_gate = back_fn(upstream * pre_up)[0].astype(jnp.bfloat16)
    feature_term = lax.dot_general(
        d_gate, full_gate, (((1,), (1,)), ((), ())), preferred_element_type=jnp.float32
    )
    feature_term = feature_term + lax.dot_general(
        d_up, full_up, (((1,), (1,)), ((), ())), preferred_element_type=jnp.float32
    )
    d_norm = lax.psum_scatter(
        feature_term.astype(jnp.bfloat16), "mp", scatter_dimension=1, tiled=True
    ).astype(jnp.float32)
    d_gain = lax.psum(jnp.sum(d_norm * scaled_rows, axis=0), "dp")
    stacked = jnp.concatenate([d_gate, d_up], axis=1)
    both = lax.psum_scatter(
        lax.dot_general(
            normed, stacked, (((0,), (0,)), ((), ())), preferred_element_type=jnp.float32
        ).astype(jnp.bfloat16),
        "dp",
        scatter_dimension=0,
        tiled=True,
    ).astype(jnp.float32)
    return (d_gain, both[:, :hidden_width], both[:, hidden_width:])


def body(tokens, norm_gain, w_gate, w_up, cotangent, decay_mask, radius):
    values = tokens.astype(jnp.float32)
    width = values.shape[1] * lax.axis_size("mp")
    row_total = lax.psum(jnp.sum(values * values, axis=1), "mp")
    scaled_rows = values * lax.rsqrt(row_total / width + 1e-06)[:, None]
    groups = decay_mask.astype(jnp.float32)
    local_rows = w_gate.shape[0]
    first_row = lax.axis_index("dp") * local_rows
    local_groups = lax.dynamic_slice_in_dim(groups, first_row, local_rows, 1)
    gate_mask = local_groups[0][:, None]
    up_mask = local_groups[1][:, None]
    full_gate, full_up = fetch_weights(w_gate, w_up)
    asc_gain, asc_gate_f, asc_up_f = one_pass(scaled_rows, norm_gain, full_gate, full_up, cotangent)
    gate_low = asc_gate_f.astype(jnp.bfloat16)
    up_low = asc_up_f.astype(jnp.bfloat16)
    gate_wide = gate_low.astype(jnp.float32)
    up_wide = up_low.astype(jnp.float32)
    matrix_part = jnp.sum(gate_mask * gate_wide * gate_wide) + jnp.sum(up_mask * up_wide * up_wide)
    total = lax.psum(matrix_part, ("dp", "mp"))
    factor = radius[0] / (jnp.sqrt(total) + 1e-12)
    new_gate = (w_gate.astype(jnp.float32) + factor * gate_mask * gate_wide).astype(jnp.bfloat16)
    new_up = (w_up.astype(jnp.float32) + factor * up_mask * up_wide).astype(jnp.bfloat16)
    next_gate, next_up = fetch_weights(new_gate, new_up)
    return one_pass(scaled_rows, norm_gain, next_gate, next_up, cotangent)


def solution(mesh):
    placed = (P("dp", "mp"), P("mp"), P("dp", "mp"), P("dp", "mp"), P("dp", "mp"), P(), P())
    return jax.shard_map(
        body,
        mesh=mesh,
        in_specs=placed,
        out_specs=(P("mp"), P("dp", "mp"), P("dp", "mp")),
        check_vma=False,
    )
```

profile of v0, /device:TPU:1, one launch (start us, length us, event | category | flops | bytes accessed | tf_op | source)
XLA Modules:
  0.0 741.6 jit_solution(15227484376641133650)
XLA Ops:
  7.2 1.0 fusion.33
  8.2 29.7 %psum.21 = f32[256]{0:T(256)S(1)} all-reduce(f32[256]{0:T(256)S(1)} %fusion.33), channel_id=1, replica_groups=mesh['dp'=16,'mp'=16] {'mp'}, use_global_device_ids=true, to_apply=%region_1.0 | all-reduce | flops 256 | bytes 2048 | tf_op jit(solution)/shard_map/psum | solution.py:53
  38.0 1.7 fusion.31
  39.7 0.7 all-gather.10.cloned.1.call-update
  40.5 0.7 all-gather.8.cloned.1.call-update
  41.2 40.3 %all-gather.6.cloned.1.call-done = bf16[256,4096]{1,0:T(8,128)(2,1)} async-done(((bf16[256,256]{1,0:T(8,128)(2,1)}), bf16[256,4096]{1,0:T(8,128)(2,1)}) %all-gather.6.cloned.1.call-update) | async-done | bytes 2097168 | tf_op jit(solution)/shard_map/all_gather | solution.py:21
  81.5 69.6 %all-gather.10.cloned.1.call-done = bf16[4096,384]{1,0:T(8,128)(2,1)} async-done(((bf16[256,384]{1,0:T(8,128)(2,1)}), bf16[4096,384]{1,0:T(8,128)(2,1)}) %all-gather.10.cloned.1.call-update) | async-done | bytes 3145744 | tf_op jit(solution)/shard_map/all_gather | solution.py:13
  151.1 3.9 fusion.21
  155.0 64.3 %all-gather.8.cloned.1.call-done = bf16[4096,384]{1,0:T(8,128)(2,1)} async-done(((bf16[256,384]{1,0:T(8,128)(2,1)}), bf16[4096,384]{1,0:T(8,128)(2,1)}) %all-gather.8.cloned.1.call-update) | async-done | bytes 3145744 | tf_op jit(solution)/shard_map/all_gather | solution.py:14
  219.4 3.3 fusion.11
  222.7 4.5 convolution_convert_fusion.1
  227.3 0.0 all-gather.14.cloned.1.call-start
  227.3 0.8 dynamic-slice_convert_fusion
  228.1 107.1 %reduce-scatter.4.cloned.1.call-done = bf16[256,768]{1,0:T(8,128)(2,1)} async-done(((bf16[4096,768]{1,0:T(8,128)(2,1)}), bf16[256,768]{1,0:T(8,128)(2,1)}) %reduce-scatter.4.cloned.1.call-update) | async-done | bytes 393232 | tf_op jit(solution)/shard_map/reduce_scatter | solution.py:39
  335.2 1.9 fusion.20
  339.0 75.6 %psum.22 = f32[]{:T(128)} all-reduce(f32[]{:T(128)S(6)} %add.55), channel_id=1, replica_groups=mesh['dp'=16,'mp'=16] {'dp','mp'}, use_global_device_ids=true, to_apply=%region_5.0 | all-reduce | flops 1 | bytes 8 | tf_op jit(solution)/shard_map/psum | solution.py:68
  415.4 2.0 fusion.4
  417.4 0.5 all-gather.12.cloned.1.call-update
  418.0 62.4 %all-gather.14.cloned.1.call-done = bf16[4096,384]{1,0:T(8,128)(2,1)} async-done(((bf16[256,384]{1,0:T(8,128)(2,1)}), bf16[4096,384]{1,0:T(8,128)(2,1)}) %all-gather.14.cloned.1.call-update) | async-done | bytes 3145744 | tf_op jit(solution)/shard_map/all_gather | solution.py:13
  480.5 3.3 fusion.22
  483.7 65.4 %all-gather.12.cloned.1.call-done = bf16[4096,384]{1,0:T(8,128)(2,1)} async-done(((bf16[256,384]{1,0:T(8,128)(2,1)}), bf16[4096,384]{1,0:T(8,128)(2,1)}) %all-gather.12.cloned.1.call-update) | async-done | bytes 3145744 | tf_op jit(solution)/shard_map/all_gather | solution.py:14
  549.1 3.5 fusion.18
  552.6 1.3 fusion.38
  553.9 0.6 copy-done.2
  554.5 2.7 fusion
  557.2 0.0 reduce-scatter.8.cloned.1.call-start
  557.3 4.5 convolution_convert_fusion
  561.8 57.3 %reduce-scatter.6.cloned.1.call-done = bf16[256,256]{1,0:T(8,128)(2,1)} async-done(((bf16[256,4096]{1,0:T(8,128)(2,1)}), bf16[256,256]{1,0:T(8,128)(2,1)}) %reduce-scatter.6.cloned.1.call-update) | async-done | bytes 131088 | tf_op jit(solution)/shard_map/reduce_scatter | solution.py:34
  619.2 1.0 fusion.32
  620.2 39.4 %psum.23 = f32[256]{0:T(256)} all-reduce(f32[256]{0:T(256)S(1)} %fusion.32), channel_id=1, replica_groups=mesh['dp'=16,'mp'=16] {'dp'}, use_global_device_ids=true, to_apply=%region_8.0 | all-reduce | flops 256 | bytes 2048 | tf_op jit(solution)/shard_map/psum | solution.py:37
  659.6 73.1 %reduce-scatter.8.cloned.1.call-done = bf16[256,768]{1,0:T(8,128)(2,1)} async-done(((bf16[4096,768]{1,0:T(8,128)(2,1)}), bf16[256,768]{1,0:T(8,128)(2,1)}) %reduce-scatter.8.cloned.1.call-update) | async-done | bytes 393232 | tf_op jit(solution)/shard_map/reduce_scatter | solution.py:39
  732.8 1.9 fusion.36
  (27 shorter events, 0.4 us)
Async XLA Ops:
  7.2 74.4 %all-gather.6.cloned.1.call-start = ((), (), s32[]{:S(2)}) async-start(), calls=%async_computation.3 | async-start | bytes 2228224 | tf_op jit(solution)/shard_map/all_gather | solution.py:21
  39.7 111.4 %all-gather.10.cloned.1.call-start = ((), (), s32[]{:S(2)}) async-start(), calls=%async_computation.5 | async-start | bytes 3342336 | tf_op jit(solution)/shard_map/all_gather | solution.py:13
  40.4 178.9 %all-gather.8.cloned.1.call-start = ((), (), s32[]{:S(2)}) async-start(), calls=%async_computation.4 | async-start | bytes 3342336 | tf_op jit(solution)/shard_map/all_gather | solution.py:14
  41.2 178.2 %copy-start.6 = (bf16[256,384]{1,0:T(8,128)(2,1)S(1)}, bf16[256,384]{1,0:T(8,128)(2,1)}, u32[]{:S(2)}) copy-start(bf16[256,384]{1,0:T(8,128)(2,1)} %param.11) | copy-start | bytes 589828
  41.2 294.1 %reduce-scatter.4.cloned.1.call-start = ((), (), s32[]{:S(2)}) async-start(), calls=%async_computation.6 | async-start | bytes 6684672 | tf_op jit(solution)/shard_map/reduce_scatter | solution.py:39
  81.5 137.8 %copy-start = (bf16[256,4096]{1,0:T(8,128)(2,1)S(1)}, bf16[256,4096]{1,0:T(8,128)(2,1)}, u32[]{:S(2)}) copy-start(bf16[256,4096]{1,0:T(8,128)(2,1)} %all-gather.6.cloned.1.call-done) | copy-start | bytes 6291460
  227.2 188.2 %copy-start.4 = (bf16[256,384]{1,0:T(8,128)(2,1)S(1)}, bf16[256,384]{1,0:T(8,128)(2,1)}, u32[]{:S(2)}) copy-start(bf16[256,384]{1,0:T(8,128)(2,1)} %param.9) | copy-start | bytes 589828
  227.2 188.2 %copy-start.5 = (bf16[256,384]{1,0:T(8,128)(2,1)S(1)}, bf16[256,384]{1,0:T(8,128)(2,1)}, u32[]{:S(2)}) copy-start(bf16[256,384]{1,0:T(8,128)(2,1)} %param.10) | copy-start | bytes 589828
  227.3 253.2 %all-gather.14.cloned.1.call-start = ((), (), s32[]{:S(2)}) async-start(), calls=%async_computation.8 | async-start | bytes 3342336 | tf_op jit(solution)/shard_map/all_gather | solution.py:13
  417.4 131.7 %all-gather.12.cloned.1.call-start = ((), (), s32[]{:S(2)}) async-start(), calls=%async_computation.7 | async-start | bytes 3342336 | tf_op jit(solution)/shard_map/all_gather | solution.py:14
  418.0 201.2 %reduce-scatter.6.cloned.1.call-start = ((), (), s32[]{:S(2)}) async-start(), calls=%async_computation.9 | async-start | bytes 2228224 | tf_op jit(solution)/shard_map/reduce_scatter | solution.py:34
  549.1 3.5 copy-start.1
  552.6 1.9 copy-start.2
  557.2 175.5 %reduce-scatter.8.cloned.1.call-start = ((), (), s32[]{:S(2)}) async-start(), calls=%async_computation.10 | async-start | bytes 6684672 | tf_op jit(solution)/shard_map/reduce_scatter | solution.py:39
  561.8 57.4 %copy-start.3 = (bf16[256,256]{1,0:T(8,128)(2,1)S(1)}, bf16[256,256]{1,0:T(8,128)(2,1)}, u32[]{:S(2)}) copy-start(bf16[256,256]{1,0:T(8,128)(2,1)} %param.7) | copy-start | bytes 393220
Sparse Core Ops, SparseCore 0:
  39.8 41.6 all-gather.5
  84.0 67.0 all-gather.9
  153.6 65.7 all-gather.7
  227.4 107.7 reduce-scatter.3
  417.5 62.9 all-gather.13
  483.4 65.7 all-gather.11
  557.3 61.7 reduce-scatter.5
  622.9 109.8 reduce-scatter.7
where the time goes:
time: 742 us
  waiting for transfers between devices  542 us (73%)
  blocking collectives  145 us (20%)
  matrix products  27.1 us (4%)
  between operations  16.9 us (2%)
  other arithmetic  8.34 us (1%)
    reduce_scatter x2, waiting for transfers between devices, one_pass(): lax.psum_scatter(lax.dot_general(normed, stacked, (((0,), (0,)), ((), ())...  180 us
    all_gather x2, waiting for transfers between devices, fetch_weights(): lax.all_gather(part_gate, 'dp', axis=0, tiled=True)  132 us
    all_gather x2, waiting for transfers between devices, fetch_weights(): lax.all_gather(part_up, 'dp', axis=0, tiled=True)  130 us
    psum x1, blocking collectives, body(): total = lax.psum(matrix_part, ('dp', 'mp'))  75.6 us
    reduce_scatter x1, waiting for transfers between devices, one_pass(): lax.psum_scatter(feature_term.astype(jnp.bfloat16), 'mp', scatter_dimensi...  57.3 us
    all_gather x1, waiting for transfers between devices, one_pass(): normed = lax.all_gather(normed_part, 'mp', axis=1, tiled=True)  40.3 us
    psum x1, blocking collectives, one_pass(): d_gain = lax.psum(jnp.sum(d_norm * scaled_rows, axis=0), 'dp')  39.4 us
    psum x1, blocking collectives, body(): row_total = lax.psum(jnp.sum(values * values, axis=1), 'mp')  29.7 us
  transfers between devices with their start and end apart: 8, of which 8 were waited for; matrix products, arithmetic and copies ran while one was open for 2% of the time, Pallas kernels for 0%

commit v1 on v0

--- a/solution.py
+++ b/solution.py
@@ -2,6 +2,16 @@
 import jax.numpy as jnp
 from jax import lax
 from jax.sharding import PartitionSpec as P
+
+teams_hold = lambda array_in: jnp.concatenate(
+    lax.all_to_all(
+        jnp.stack([array_in] * lax.axis_size("dp"), axis=0),
+        axis_name="dp",
+        split_axis=0,
+        concat_axis=0,
+    ),
+    axis=0,
+)
 
 
 def activation(value):
@@ -9,10 +19,7 @@
 
 
 def fetch_weights(part_gate, part_up):
-    return (
-        lax.all_gather(part_gate, "dp", axis=0, tiled=True),
-        lax.all_gather(part_up, "dp", axis=0, tiled=True),
-    )
+    return (teams_hold(part_gate), lax.all_gather(part_up, "dp", axis=0, tiled=True))
 
 
 def one_pass(scaled_rows, gain_part, full_gate, full_up, cotangent):

time: 742 us -> 687 us (0.926)
  waiting for transfers between devices: 542 us -> 463 us
  starting transfers between devices: 0.32 us -> 14.7 us
    all_gather x2 -> x0, waiting for transfers between devices: 132 us -> none  [fetch_weights(): lax.all_gather(part_gate, 'dp', axis=0, tiled=True)]
    all_to_all x0 -> x2, waiting for transfers between devices: none -> 96.7 us  [lax.all_to_all(jnp.stack([array_in] * lax.axis_size('dp'), axis=0), axis_...]
    all_gather x2, waiting for transfers between devices: 130 us -> 74.8 us  [fetch_weights(): lax.all_gather(part_up, 'dp', axis=0, tiled=True)]
    all_to_all x0 -> x2, starting transfers between devices: none -> 14.3 us  [lax.all_to_all(jnp.stack([array_in] * lax.axis_size('dp'), axis=0), axis_...]
    all_gather x1, waiting for transfers between devices: 40.3 us -> 52.5 us  [one_pass(): normed = lax.all_gather(normed_part, 'mp', axis=1, tiled=True)]
where the time goes in v1:
time: 687 us; the launch traced here: 686 us
  waiting for transfers between devices  463 us (67%)
  blocking collectives  145 us (21%)
  matrix products  29.2 us (4%)
  between operations  16.9 us (2%)
  starting transfers between devices  14.7 us (2%)
  local copies, waits for them, and re-layouts  8.78 us (1%)
  other arithmetic  8.19 us (1%)
    reduce_scatter x2, waiting for transfers between devices, one_pass(): lax.psum_scatter(lax.dot_general(normed, stacked, (((0,), (0,)), ((), ())...  180 us
    all_to_all x2, waiting for transfers between devices, lax.all_to_all(jnp.stack([array_in] * lax.axis_size('dp'), axis=0), axis_...  96.7 us
    psum x1, blocking collectives, body(): total = lax.psum(matrix_part, ('dp', 'mp'))  75.6 us
    all_gather x2, waiting for transfers between devices, fetch_weights(): lax.all_gather(part_up, 'dp', axis=0, tiled=True)  74.8 us
    reduce_scatter x1, waiting for transfers between devices, one_pass(): lax.psum_scatter(feature_term.astype(jnp.bfloat16), 'mp', scatter_dimensi...  58.2 us
    all_gather x1, waiting for transfers between devices, one_pass(): normed = lax.all_gather(normed_part, 'mp', axis=1, tiled=True)  52.5 us
    psum x1, blocking collectives, one_pass(): d_gain = lax.psum(jnp.sum(d_norm * scaled_rows, axis=0), 'dp')  39.7 us
    psum x1, blocking collectives, body(): row_total = lax.psum(jnp.sum(values * values, axis=1), 'mp')  29.7 us
  transfers between devices with their start and end apart: 8, of which 8 were waited for; matrix products, arithmetic and copies ran while one was open for 2% of the time, Pallas kernels for 0%

profile of v1, /device:TPU:1, one launch (start us, length us, event | category | flops | bytes accessed | tf_op | source)
XLA Modules:
  0.0 686.1 jit_solution(17362352662696367271)
XLA Ops:
  7.2 1.0 fusion.33
  8.2 29.7 %psum.21 = f32[256]{0:T(256)S(1)} all-reduce(f32[256]{0:T(256)S(1)} %fusion.33), channel_id=1, replica_groups=mesh['dp'=16,'mp'=16] {'mp'}, use_global_device_ids=true, to_apply=%region_1.0 | all-reduce | flops 256 | bytes 2048 | tf_op jit(solution)/shard_map/psum | solution.py:60
  38.0 1.7 fusion.31
  39.7 3.0 stack.4
  42.7 9.3 %all-to-all-start = ((bf16[16,256,384]{2,1,0:T(8,128)(2,1)}), bf16[16,256,384]{2,1,0:T(8,128)(2,1)S(1)}, u32[]{:S(2)}, u32[]{:S(2)}) async-start(bf16[16,256,384]{2,1,0:T(8,128)(2,1)} %stack.4), calls=%async_computation | async-start | bytes 6291456 | tf_op jit(solution)/shard_map/all_to_all | solution.py:7
  52.1 0.7 all-gather.6.cloned.1.call-update
  52.8 52.5 %all-gather.4.cloned.1.call-done = bf16[256,4096]{1,0:T(8,128)(2,1)} async-done(((bf16[256,256]{1,0:T(8,128)(2,1)}), bf16[256,4096]{1,0:T(8,128)(2,1)}) %all-gather.4.cloned.1.call-update) | async-done | bytes 2097168 | tf_op jit(solution)/shard_map/all_gather | solution.py:28
  105.3 28.8 %all-to-all-done = bf16[16,256,384]{2,1,0:T(8,128)(2,1)S(1)} async-done(((bf16[16,256,384]{2,1,0:T(8,128)(2,1)}), bf16[16,256,384]{2,1,0:T(8,128)(2,1)S(1)}, u32[]{:S(2)}, u32[]{:S(2)}) %all-to-all-start) | async-done | bytes 3145760 | tf_op jit(solution)/shard_map/all_to_all | solution.py:7
  134.1 1.7 copy-done.1
  135.8 4.0 fusion.21
  139.8 42.0 %all-gather.6.cloned.1.call-done = bf16[4096,384]{1,0:T(8,128)(2,1)} async-done(((bf16[256,384]{1,0:T(8,128)(2,1)}), bf16[4096,384]{1,0:T(8,128)(2,1)}) %all-gather.6.cloned.1.call-update) | async-done | bytes 3145744 | tf_op jit(solution)/shard_map/all_gather | solution.py:22
  181.8 3.3 fusion.11
  185.2 4.5 convolution_convert_fusion.1
  189.7 0.7 dynamic-slice_convert_fusion
  190.5 106.9 %reduce-scatter.4.cloned.1.call-done = bf16[256,768]{1,0:T(8,128)(2,1)} async-done(((bf16[4096,768]{1,0:T(8,128)(2,1)}), bf16[256,768]{1,0:T(8,128)(2,1)}) %reduce-scatter.4.cloned.1.call-update) | async-done | bytes 393232 | tf_op jit(solution)/shard_map/reduce_scatter | solution.py:46
  297.3 1.9 fusion.20
  301.2 75.6 %psum.22 = f32[]{:T(128)} all-reduce(f32[]{:T(128)S(6)} %add.55), channel_id=1, replica_groups=mesh['dp'=16,'mp'=16] {'dp','mp'}, use_global_device_ids=true, to_apply=%region_5.0 | all-reduce | flops 1 | bytes 8 | tf_op jit(solution)/shard_map/psum | solution.py:75
  377.5 1.9 fusion.4
  379.4 2.1 stack.5
  381.5 5.0 all-to-all-start.1
  387.2 67.9 %all-to-all-done.1 = bf16[16,256,384]{2,1,0:T(8,128)(2,1)} async-done(((bf16[16,256,384]{2,1,0:T(8,128)(2,1)}), bf16[16,256,384]{2,1,0:T(8,128)(2,1)}, u32[]{:S(2)}, u32[]{:S(2)}) %all-to-all-start.1) | async-done | bytes 3145760 | tf_op jit(solution)/shard_map/all_to_all | solution.py:7
  455.2 3.4 fusion.22
  458.6 32.7 %all-gather.8.cloned.1.call-done = bf16[4096,384]{1,0:T(8,128)(2,1)} async-done(((bf16[256,384]{1,0:T(8,128)(2,1)}), bf16[4096,384]{1,0:T(8,128)(2,1)}) %all-gather.8.cloned.1.call-update) | async-done | bytes 3145744 | tf_op jit(solution)/shard_map/all_gather | solution.py:22
  491.3 3.3 fusion.18
  494.7 3.3 fusion.38
  498.0 2.7 fusion
  500.8 4.5 convolution_convert_fusion
  505.3 58.2 %reduce-scatter.6.cloned.1.call-done = bf16[256,256]{1,0:T(8,128)(2,1)} async-done(((bf16[256,4096]{1,0:T(8,128)(2,1)}), bf16[256,256]{1,0:T(8,128)(2,1)}) %reduce-scatter.6.cloned.1.call-update) | async-done | bytes 131088 | tf_op jit(solution)/shard_map/reduce_scatter | solution.py:41
  563.5 1.0 fusion.32
  564.6 39.7 %psum.23 = f32[256]{0:T(256)} all-reduce(f32[256]{0:T(256)S(1)} %fusion.32), channel_id=1, replica_groups=mesh['dp'=16,'mp'=16] {'dp'}, use_global_device_ids=true, to_apply=%region_8.0 | all-reduce | flops 256 | bytes 2048 | tf_op jit(solution)/shard_map/psum | solution.py:44
  604.3 73.1 %reduce-scatter.8.cloned.1.call-done = bf16[256,768]{1,0:T(8,128)(2,1)} async-done(((bf16[4096,768]{1,0:T(8,128)(2,1)}), bf16[256,768]{1,0:T(8,128)(2,1)}) %reduce-scatter.8.cloned.1.call-update) | async-done | bytes 393232 | tf_op jit(solution)/shard_map/reduce_scatter | solution.py:46
  677.4 1.9 fusion.36
  (27 shorter events, 1.1 us)
Async XLA Ops:
  7.2 98.1 %all-gather.4.cloned.1.call-start = ((), (), s32[]{:S(2)}) async-start(), calls=%async_computation.5 | async-start | bytes 2228224 | tf_op jit(solution)/shard_map/all_gather | solution.py:28
  42.7 93.1 %copy-start.6 = (bf16[256,384]{1,0:T(8,128)(2,1)S(1)}, bf16[256,384]{1,0:T(8,128)(2,1)}, u32[]{:S(2)}) copy-start(bf16[256,384]{1,0:T(8,128)(2,1)} %param.11) | copy-start | bytes 589828
  42.7 91.4 %all-to-all-start = ((bf16[16,256,384]{2,1,0:T(8,128)(2,1)}), bf16[16,256,384]{2,1,0:T(8,128)(2,1)S(1)}, u32[]{:S(2)}, u32[]{:S(2)}) async-start(bf16[16,256,384]{2,1,0:T(8,128)(2,1)} %stack.4), calls=%async_computation | async-start | bytes 6291456 | tf_op jit(solution)/shard_map/all_to_all | solution.py:7
  52.0 129.8 %all-gather.6.cloned.1.call-start = ((), (), s32[]{:S(2)}) async-start(), calls=%async_computation.6 | async-start | bytes 3342336 | tf_op jit(solution)/shard_map/all_gather | solution.py:22
  52.8 244.6 %reduce-scatter.4.cloned.1.call-start = ((), (), s32[]{:S(2)}) async-start(), calls=%async_computation.7 | async-start | bytes 6684672 | tf_op jit(solution)/shard_map/reduce_scatter | solution.py:46
  134.1 1.7 copy-start.1
  135.8 46.1 %copy-start = (bf16[256,4096]{1,0:T(8,128)(2,1)S(1)}, bf16[256,4096]{1,0:T(8,128)(2,1)}, u32[]{:S(2)}) copy-start(bf16[256,4096]{1,0:T(8,128)(2,1)} %all-gather.4.cloned.1.call-done) | copy-start | bytes 6291460
  189.7 187.8 %copy-start.4 = (bf16[256,384]{1,0:T(8,128)(2,1)S(1)}, bf16[256,384]{1,0:T(8,128)(2,1)}, u32[]{:S(2)}) copy-start(bf16[256,384]{1,0:T(8,128)(2,1)} %param.9) | copy-start | bytes 589828
  189.7 187.8 %copy-start.5 = (bf16[256,384]{1,0:T(8,128)(2,1)S(1)}, bf16[256,384]{1,0:T(8,128)(2,1)}, u32[]{:S(2)}) copy-start(bf16[256,384]{1,0:T(8,128)(2,1)} %param.10) | copy-start | bytes 589828
  381.5 73.7 %all-to-all-start.1 = ((bf16[16,256,384]{2,1,0:T(8,128)(2,1)}), bf16[16,256,384]{2,1,0:T(8,128)(2,1)}, u32[]{:S(2)}, u32[]{:S(2)}) async-start(bf16[16,256,384]{2,1,0:T(8,128)(2,1)} %stack.5), calls=%async_computation.2 | async-start | bytes 6291456 | tf_op jit(solution)/shard_map/all_to_all | solution.py:7
  386.4 104.9 %all-gather.8.cloned.1.call-start = ((), (), s32[]{:S(2)}) async-start(), calls=%async_computation.8 | async-start | bytes 3342336 | tf_op jit(solution)/shard_map/all_gather | solution.py:22
  387.0 176.5 %reduce-scatter.6.cloned.1.call-start = ((), (), s32[]{:S(2)}) async-start(), calls=%async_computation.9 | async-start | bytes 2228224 | tf_op jit(solution)/shard_map/reduce_scatter | solution.py:41
  494.7 3.3 copy-start.2
  500.7 176.6 %reduce-scatter.8.cloned.1.call-start = ((), (), s32[]{:S(2)}) async-start(), calls=%async_computation.10 | async-start | bytes 6684672 | tf_op jit(solution)/shard_map/reduce_scatter | solution.py:46
  505.3 58.2 %copy-start.3 = (bf16[256,256]{1,0:T(8,128)(2,1)S(1)}, bf16[256,256]{1,0:T(8,128)(2,1)}, u32[]{:S(2)}) copy-start(bf16[256,256]{1,0:T(8,128)(2,1)} %param.7) | copy-start | bytes 393220
Sparse Core Ops, SparseCore 0:
  39.8 65.4 all-gather.3
  107.8 74.0 all-gather.5
  189.8 107.4 reduce-scatter.3
  390.0 101.2 all-gather.7
  500.8 62.6 reduce-scatter.5
  567.1 110.1 reduce-scatter.7
